TPU v7x, 32 devices: a whole 2x2x4 slice. The times are simulated.
32 devices in a mesh: rep: 16 (over z, y, core), tp: 2 (over x).
Axes of the slice: x: 2, y: 2, z: 4, core: 2. Of those that a mesh axis runs over, the one named last changes fastest.
Arguments:
- queries: bfloat16 [4096, 8192], P('rep', 'tp'), may hold values from -8 to 8
- cand_keys: bfloat16 [4096, 1024], P('rep', 'tp'), may hold values from -6 to 6
- cand_values: bfloat16 [4096, 1024], P('rep', 'tp'), may hold values from -6 to 6
- prefix_kv: bfloat16 [16, 2, 4096, 1024], P('rep', None, None, 'tp'), may hold values from -8 to 8
- owner: int32 [1], replicated, may hold values from 0 to 15
- lengths: int32 [16, 2], P('rep'), may hold values from 1 to 128, as said below
- out_weight: bfloat16 [8192, 4096], P('tp'), may hold values from -2.390625 to 2.390625
Outputs:
- attn_out: bfloat16 [4096, 4096], P(('rep', 'tp'))
Inputs may be any that keep to these rules, and one draw needn't show every extreme that they name: Only the slice of prefix_kv at index owner[0] is read. Candidate c of group g has its real tokens in its first lengths[g, c] slots; the rest are padding.
All inputs are finite; a program needn't handle non-finite values.
Results may differ from a plain program's by a relative error of at most 0.017.
Values may be sent and summed in bfloat16 or wider, within the bound.
A program may use at most 192 MiB of HBM per device.

v0:
```python
import math

import jax
import jax.numpy as jnp
from jax import lax
from jax.sharding import PartitionSpec as P

QH = 64
KVH = 8
HD = 128
CLEN = 128


NEG = -1e30


def broadcast(shard, axis, root):
    mine = lax.axis_index(axis) == root
    return lax.psum(jnp.where(mine, shard, jnp.zeros_like(shard)), axis)


def body(queries, cand_keys, cand_values, prefix_kv, owner, lengths, out_weight):
    row_count = queries.shape[0]
    kv_heads = cand_keys.shape[1] // HD
    head_group = QH // KVH
    cand_count = row_count // CLEN
    score_scale = 1.0 / math.sqrt(HD)
    query_grid = queries.reshape(row_count, kv_heads, head_group, HD)
    cand_queries = queries.reshape(cand_count, CLEN, kv_heads, head_group, HD)
    key_grid = cand_keys.reshape(cand_count, CLEN, kv_heads, HD)
    value_grid = cand_values.reshape(cand_count, CLEN, kv_heads, HD)
    own_scores = (
        jnp.einsum("cikgd,cjkd->kgcij", cand_queries, key_grid, preferred_element_type=jnp.float32)
        * score_scale
    )
    live_mask = jnp.arange(CLEN, dtype=jnp.int32)[None, :] < lengths[0][:, None]
    own_scores = jnp.where(live_mask[None, None, :, None, :], own_scores, NEG)
    own_max = jnp.max(own_scores, -1)
    exponent = jnp.exp(own_scores - own_max[..., None])
    row_total = jnp.sum(exponent, -1).reshape(kv_heads, head_group, row_count)
    weighted = jnp.einsum(
        "kgcij,cjkd->kgcid",
        exponent.astype(jnp.bfloat16),
        value_grid,
        preferred_element_type=jnp.float32,
    )
    weighted = weighted.reshape(kv_heads, head_group, row_count, HD)
    row_max = own_max.reshape(kv_heads, head_group, row_count)

    def absorb(running, block_keys, block_values):
        old_max, old_total, old_weighted = running
        block_width = block_keys.shape[0]
        scores = (
            jnp.einsum(
                "xlpm,vlm->lpxv",
                query_grid,
                block_keys.reshape(block_width, kv_heads, HD),
                preferred_element_type=jnp.float32,
            )
            * score_scale
        )
        new_max = jnp.maximum(old_max, jnp.max(scores, -1))
        factor = jnp.exp(old_max - new_max)
        block_expo = jnp.exp(scores - new_max[..., None])
        new_total = old_total * factor + jnp.sum(block_expo, -1)
        new_weighted = old_weighted * factor[..., None] + jnp.einsum(
            "ipuo,oit->iput",
            block_expo.astype(jnp.bfloat16),
            block_values.reshape(block_width, kv_heads, HD),
            preferred_element_type=jnp.float32,
        )
        return (new_max, new_total, new_weighted)

    prefix_len = prefix_kv.shape[2]
    block_width = min(1024, prefix_len)
    block_count = prefix_len // block_width
    owner_index = owner[0]
    own_prefix = prefix_kv[0]
    arrived = broadcast(own_prefix, "rep", owner_index)

    def advance(block_index, running):
        prefix_piece = lax.dynamic_slice_in_dim(arrived, block_index * block_width, block_width, 1)
        return absorb(running, prefix_piece[0], prefix_piece[1])

    row_max, row_total, weighted = lax.fori_loop(
        0, block_count, advance, (row_max, row_total, weighted)
    )
    context = weighted / row_total[..., None]
    context = (
        jnp.transpose(context, (2, 0, 1, 3))
        .reshape(row_count, kv_heads * head_group * HD)
        .astype(jnp.bfloat16)
    )
    return lax.psum_scatter(
        jnp.dot(context, out_weight, preferred_element_type=jnp.float32).astype(jnp.bfloat16),
        "tp",
        scatter_dimension=0,
        tiled=True,
    )


def solution(mesh):
    in_specs = (
        P("rep", "tp"),
        P("rep", "tp"),
        P("rep", "tp"),
        P("rep", None, None, "tp"),
        P(),
        P("rep", None),
        P("tp", None),
    )
    out_specs = P(("rep", "tp"), None)
    return jax.shard_map(body, mesh=mesh, in_specs=in_specs, out_specs=out_specs, check_vma=False)
```

profile of v0, /device:TPU:0, one launch (start us, length us, event | category | flops | bytes accessed | tf_op | source)
XLA Modules:
  0.0 439.4 jit_solution(14652065497964288879)
XLA Ops:
  7.2 12.1 %copy.21 = bf16[1,2,4096,512]{2,3,1,0:T(8,128)(2,1)} copy(bf16[1,2,4096,512]{3,2,1,0:T(8,128)(2,1)} %param.12) | data formatting | bytes 16777216 | tf_op args[3]
  19.3 3.8 select_bitcast_fusion
  24.8 2.5 copy.22
  31.2 2.9 copy.20
  34.1 3.0 copy.23
  37.1 3.4 fusion.12
  40.5 156.9 %all-reduce.2.cloned.1.call-done = bf16[2,4096,512]{1,2,0:T(8,128)(2,1)} async-done(((bf16[2,4096,512]{1,2,0:T(8,128)(2,1)}), bf16[2,4096,512]{1,2,0:T(8,128)(2,1)}) %all-reduce.2.cloned.1.call-update) | async-done | bytes 8388624 | tf_op jit(solution)/shard_map/psum | solution.py:19
  197.4 178.3 %while.17 = (s32[]{:T(128)}, f32[4,8,256]{2,1,0:T(8,128)S(1)}, f32[4,8,256]{2,1,0:T(8,128)S(1)}, f32[4,8,256,128]{3,2,1,0:T(8,128)}, bf16[2,4096,512]{1,2,0:T(8,...) while((s32[]{:T(128)}, f32[4,8,256]{2,1,0:T(8,128)S(1)}, ...), condition=%wide.region_6.7_spmd, body=%wide.region_3.6_spmd.sunk | while | flops 4364189696 | bytes 151519472 | solution.py:85
  199.1 13.1 %bitcast_reduce_fusion.3 = (f32[4,8,256]{2,1,0:T(8,128)S(1)}, f32[4,1024,256,8]{2,1,3,0:T(8,128)}) fusion(bf16[1024,4,128,1]{0,2,3,1:T(8,128)(2,1)S(1)} %bitcast.74, bf16[256,4,8,128]{3,0,2,1:T(8,128)(2,1)S(1)} %get-tuple-element.219), kind=kOutput, calls=%fused_computation.1.clone.1 | convolution fusion | flops 2164252672 | bytes 36732928 | tf_op jit(solution)/shard_map/while/body/eval_jaxpr/xlpm,vlm->lpxv/dot_general | solution.py:54
  212.2 13.7 %fusion.38 = f32[4,8,256]{2,1,0:T(8,128)S(1)} fusion(f32[4,1024,256,8]{2,1,3,0:T(8,128)} %get-tuple-element.188, f32[4,8,256]{2,1,0:T(8,128)S(1)} %max.8), kind=kLoop, calls=%fused_computation.4.clone.1 | loop fusion | flops 25157632 | bytes 33619968 | tf_op jit(solution)/shard_map/while/body/eval_jaxpr/reduce_sum | solution.py:65
  226.0 14.0 %multiply_add_fusion.5 = f32[4,8,256,128]{3,2,1,0:T(8,128)S(1)} fusion(f32[4,8,256,128]{3,2,1,0:T(8,128)S(1)} %copy-done, bf16[1024,4,128,1]{0,2,3,1:T(8,128)(2,1)S(1)} %bitcast.73, f32[4,1024,256,8]{2,1,3,0:T(8,128)} %get-tuple-element.188, f32[4,8,256]{2,1,0:T(8,128)S(1)} %max.8, f32[4,8,256]{2,1,0:T(8,128)S(1)} %get-tuple-element.191), kind=kOutput, calls=%fused_computation.8.clone.1 | convolution fusion | flops 2174746624 | bytes 43057152 | tf_op jit(solution)/shard_map/while/body/eval_jaxpr/ipuo,oit->iput/dot_general | solution.py:66
  243.6 13.1 %bitcast_reduce_fusion.3 = (f32[4,8,256]{2,1,0:T(8,128)S(1)}, f32[4,1024,256,8]{2,1,3,0:T(8,128)}) fusion(bf16[1024,4,128,1]{0,2,3,1:T(8,128)(2,1)S(1)} %bitcast.74, bf16[256,4,8,128]{3,0,2,1:T(8,128)(2,1)S(1)} %get-tuple-element.219), kind=kOutput, calls=%fused_computation.1.clone.1 | convolution fusion | flops 2164252672 | bytes 36732928 | tf_op jit(solution)/shard_map/while/body/eval_jaxpr/xlpm,vlm->lpxv/dot_general | solution.py:54
  256.8 13.7 %fusion.38 = f32[4,8,256]{2,1,0:T(8,128)S(1)} fusion(f32[4,1024,256,8]{2,1,3,0:T(8,128)} %get-tuple-element.188, f32[4,8,256]{2,1,0:T(8,128)S(1)} %max.8), kind=kLoop, calls=%fused_computation.4.clone.1 | loop fusion | flops 25157632 | bytes 33619968 | tf_op jit(solution)/shard_map/while/body/eval_jaxpr/reduce_sum | solution.py:65
  270.5 14.0 %multiply_add_fusion.5 = f32[4,8,256,128]{3,2,1,0:T(8,128)S(1)} fusion(f32[4,8,256,128]{3,2,1,0:T(8,128)S(1)} %copy-done, bf16[1024,4,128,1]{0,2,3,1:T(8,128)(2,1)S(1)} %bitcast.73, f32[4,1024,256,8]{2,1,3,0:T(8,128)} %get-tuple-element.188, f32[4,8,256]{2,1,0:T(8,128)S(1)} %max.8, f32[4,8,256]{2,1,0:T(8,128)S(1)} %get-tuple-element.191), kind=kOutput, calls=%fused_computation.8.clone.1 | convolution fusion | flops 2174746624 | bytes 43057152 | tf_op jit(solution)/shard_map/while/body/eval_jaxpr/ipuo,oit->iput/dot_general | solution.py:66
  288.2 13.1 %bitcast_reduce_fusion.3 = (f32[4,8,256]{2,1,0:T(8,128)S(1)}, f32[4,1024,256,8]{2,1,3,0:T(8,128)}) fusion(bf16[1024,4,128,1]{0,2,3,1:T(8,128)(2,1)S(1)} %bitcast.74, bf16[256,4,8,128]{3,0,2,1:T(8,128)(2,1)S(1)} %get-tuple-element.219), kind=kOutput, calls=%fused_computation.1.clone.1 | convolution fusion | flops 2164252672 | bytes 36732928 | tf_op jit(solution)/shard_map/while/body/eval_jaxpr/xlpm,vlm->lpxv/dot_general | solution.py:54
  301.3 13.7 %fusion.38 = f32[4,8,256]{2,1,0:T(8,128)S(1)} fusion(f32[4,1024,256,8]{2,1,3,0:T(8,128)} %get-tuple-element.188, f32[4,8,256]{2,1,0:T(8,128)S(1)} %max.8), kind=kLoop, calls=%fused_computation.4.clone.1 | loop fusion | flops 25157632 | bytes 33619968 | tf_op jit(solution)/shard_map/while/body/eval_jaxpr/reduce_sum | solution.py:65
  315.1 14.0 %multiply_add_fusion.5 = f32[4,8,256,128]{3,2,1,0:T(8,128)S(1)} fusion(f32[4,8,256,128]{3,2,1,0:T(8,128)S(1)} %copy-done, bf16[1024,4,128,1]{0,2,3,1:T(8,128)(2,1)S(1)} %bitcast.73, f32[4,1024,256,8]{2,1,3,0:T(8,128)} %get-tuple-element.188, f32[4,8,256]{2,1,0:T(8,128)S(1)} %max.8, f32[4,8,256]{2,1,0:T(8,128)S(1)} %get-tuple-element.191), kind=kOutput, calls=%fused_computation.8.clone.1 | convolution fusion | flops 2174746624 | bytes 43057152 | tf_op jit(solution)/shard_map/while/body/eval_jaxpr/ipuo,oit->iput/dot_general | solution.py:66
  332.8 13.1 %bitcast_reduce_fusion.3 = (f32[4,8,256]{2,1,0:T(8,128)S(1)}, f32[4,1024,256,8]{2,1,3,0:T(8,128)}) fusion(bf16[1024,4,128,1]{0,2,3,1:T(8,128)(2,1)S(1)} %bitcast.74, bf16[256,4,8,128]{3,0,2,1:T(8,128)(2,1)S(1)} %get-tuple-element.219), kind=kOutput, calls=%fused_computation.1.clone.1 | convolution fusion | flops 2164252672 | bytes 36732928 | tf_op jit(solution)/shard_map/while/body/eval_jaxpr/xlpm,vlm->lpxv/dot_general | solution.py:54
  345.9 13.7 %fusion.38 = f32[4,8,256]{2,1,0:T(8,128)S(1)} fusion(f32[4,1024,256,8]{2,1,3,0:T(8,128)} %get-tuple-element.188, f32[4,8,256]{2,1,0:T(8,128)S(1)} %max.8), kind=kLoop, calls=%fused_computation.4.clone.1 | loop fusion | flops 25157632 | bytes 33619968 | tf_op jit(solution)/shard_map/while/body/eval_jaxpr/reduce_sum | solution.py:65
  359.7 14.0 %multiply_add_fusion.5 = f32[4,8,256,128]{3,2,1,0:T(8,128)S(1)} fusion(f32[4,8,256,128]{3,2,1,0:T(8,128)S(1)} %copy-done, bf16[1024,4,128,1]{0,2,3,1:T(8,128)(2,1)S(1)} %bitcast.73, f32[4,1024,256,8]{2,1,3,0:T(8,128)} %get-tuple-element.188, f32[4,8,256]{2,1,0:T(8,128)S(1)} %max.8, f32[4,8,256]{2,1,0:T(8,128)S(1)} %get-tuple-element.191), kind=kOutput, calls=%fused_computation.8.clone.1 | convolution fusion | flops 2174746624 | bytes 43057152 | tf_op jit(solution)/shard_map/while/body/eval_jaxpr/ipuo,oit->iput/dot_general | solution.py:66
  375.6 5.4 %copy.24 = f32[4,8,256,128]{2,3,1,0:T(8,128)} copy(f32[4,8,256,128]{3,2,1,0:T(8,128)} %get-tuple-element.115) | data formatting | bytes 8388608 | tf_op jit(solution)/shard_map/while | solution.py:85
  381.0 2.7 divide_convert_fusion
  383.7 16.9 %convolution_convert_fusion = bf16[256,4096]{1,0:T(8,128)(2,1)} fusion(bf16[256,4096]{0,1:T(8,128)(2,1)S(1)} %bitcast.75, bf16[4096,4096]{1,0:T(8,128)(2,1)} %param.15), kind=kOutput, calls=%fused_computation.15 | convolution fusion | flops 8590983168 | bytes 37748736 | tf_op jit(solution)/shard_map/dot_general | solution.py:95
  400.6 31.9 %reduce-scatter.2.cloned.1.call-done = bf16[128,4096]{1,0:T(8,128)(2,1)} async-done(((bf16[256,4096]{1,0:T(8,128)(2,1)}), bf16[128,4096]{1,0:T(8,128)(2,1)}) %reduce-scatter.2.cloned.1.call-update) | async-done | bytes 1048592 | tf_op jit(solution)/shard_map/reduce_scatter | solution.py:94
  (52 shorter events, 20.3 us)
Async XLA Ops:
  6.5 190.8 %all-reduce.2.cloned.1.call-start = ((), (), s32[]{:S(2)}) async-start(), calls=%async_computation.1 | async-start | bytes 16777216 | tf_op jit(solution)/shard_map/psum | solution.py:19
  23.0 0.9 copy-start.4
  23.0 1.0 copy-start.5
  23.0 1.8 copy-start.3
  23.1 409.5 %reduce-scatter.2.cloned.1.call-start = ((), (), s32[]{:S(2)}) async-start(), calls=%async_computation.2 | async-start | bytes 3145728 | tf_op jit(solution)/shard_map/reduce_scatter | solution.py:94
  24.8 3.0 copy-start.6
  29.2 2.0 copy-start.2
  212.2 13.7 %copy-start = (f32[4,8,256,128]{3,2,1,0:T(8,128)S(1)}, f32[4,8,256,128]{3,2,1,0:T(8,128)}, u32[]{:S(2)}) copy-start(f32[4,8,256,128]{3,2,1,0:T(8,128)} %get-tuple-element.206) | copy-start | bytes 12582916 | tf_op jit(solution)/shard_map/while
  240.0 1.9 copy-start.1
  256.8 13.7 %copy-start = (f32[4,8,256,128]{3,2,1,0:T(8,128)S(1)}, f32[4,8,256,128]{3,2,1,0:T(8,128)}, u32[]{:S(2)}) copy-start(f32[4,8,256,128]{3,2,1,0:T(8,128)} %get-tuple-element.206) | copy-start | bytes 12582916 | tf_op jit(solution)/shard_map/while
  284.6 1.9 copy-start.1
  301.3 13.7 %copy-start = (f32[4,8,256,128]{3,2,1,0:T(8,128)S(1)}, f32[4,8,256,128]{3,2,1,0:T(8,128)}, u32[]{:S(2)}) copy-start(f32[4,8,256,128]{3,2,1,0:T(8,128)} %get-tuple-element.206) | copy-start | bytes 12582916 | tf_op jit(solution)/shard_map/while
  329.1 1.9 copy-start.1
  345.9 13.7 %copy-start = (f32[4,8,256,128]{3,2,1,0:T(8,128)S(1)}, f32[4,8,256,128]{3,2,1,0:T(8,128)}, u32[]{:S(2)}) copy-start(f32[4,8,256,128]{3,2,1,0:T(8,128)} %get-tuple-element.206) | copy-start | bytes 12582916 | tf_op jit(solution)/shard_map/while
  373.7 1.9 copy-start.1
Sparse Core Ops, SparseCore 0:
  23.2 174.1 all-reduce.1
  400.7 31.7 reduce-scatter.1
where the time goes:
time: 440 us; the launch traced here: 439 us
  waiting for transfers between devices  189 us (43%)
  matrix products  128 us (29%)
  other arithmetic  64.8 us (15%)
  local copies, waits for them, and re-layouts  43.2 us (10%)
  between operations  14.1 us (3%)
    psum x1, waiting for transfers between devices, broadcast(): return lax.psum(jnp.where(mine, shard, jnp.zeros_like(shard)), axis)  157 us
    dot_general x4, matrix products, absorb(): jnp.einsum('ipuo,oit->iput', block_expo.astype(jnp.bfloat16), block_value...  56.1 us
    reduce_sum x4, other arithmetic, absorb(): new_total = old_total * factor + jnp.sum(block_expo, -1)  54.8 us
    dot_general x4, matrix products, absorb(): jnp.einsum('xlpm,vlm->lpxv', query_grid, block_keys.reshape(block_width,...  52.5 us
    reduce_scatter x1, waiting for transfers between devices, body(): lax.psum_scatter(jnp.dot(context, out_weight, preferred_element_type=jnp....  31.9 us
    unnamed x13, local copies, waits for them, and re-layouts  17.2 us
    dot_general x1, matrix products, body(): jnp.dot(context, out_weight, preferred_element_type=jnp.float32)  16.9 us
  transfers between devices with their start and end apart: 2, of which 2 were waited for; matrix products, arithmetic and copies ran while one was open for 3% of the time, Pallas kernels for 0%

commit v1 on v0

v1 whole, which is shorter than its diff:
```python
import functools
import math

import jax
import jax.numpy as jnp
from jax import lax
from jax.experimental import pallas as pl
from jax.experimental.pallas import tpu as pltpu
from jax.sharding import PartitionSpec as P

QH = 64
KVH = 8
HD = 128
CLEN = 128
NEG = -1e30
MESH = pl.DeviceIdType.MESH


def plan(root, ranks):
    chips = ranks // 2
    lines = chips // 2
    rz, ry = (root // 2) // 2, (root // 2) % 2
    oy = 1 - ry
    rank = lambda z, y, c: (z * 2 + y) * 2 + c
    passes = [[] for _ in range(ranks)]
    sib = root ^ 1

    def edge(s, src, dst):
        source = root if src == (rz, ry) else rank(*src, s)
        passes[source].append((s, rank(*dst, s)))

    for s, row in ((0, ry), (1, oy)):
        for z in range(rz, lines - 1):
            edge(s, (z, row), (z + 1, row))
        for z in range(rz, 0, -1):
            edge(s, (z, row), (z - 1, row))
        for z in range(lines):
            if z != rz:
                edge(s, (z, row), (z, 1 - row))
    back = rz + 1 if rz + 1 < lines else rz - 1
    edge(0, (back, oy), (rz, oy))
    edge(1, (rz, ry), (rz, oy))
    for i in range(ranks):
        if i == root:
            passes[i] += [(0, sib), (1, sib)]
        elif i == sib:
            passes[i] += [(0, root), (1, root)]
        else:
            passes[i].append((i % 2, i ^ 1))
    return passes


def bcast_kernel(root, ranks, chunks, x_ref, o_ref, send_sem, recv_sem):
    me = lax.axis_index("rep")
    passes = plan(root, ranks)
    half = x_ref.shape[1] // 2
    width = half // chunks
    near = [set(t for _, t in passes[i]) for i in range(ranks)]
    for i in range(ranks):
        for t in list(near[i]):
            near[t].add(i)

    def piece(ref, s, k):
        return ref.at[:, pl.ds(pl.multiple_of(s * half + k * width, width), width), :]

    def copy(ref, s, k, slot, target):
        return pltpu.make_async_remote_copy(
            src_ref=piece(ref, s, k),
            dst_ref=piece(o_ref, s, k),
            send_sem=send_sem.at[slot],
            recv_sem=recv_sem.at[s, k],
            device_id={"rep": target},
            device_id_type=MESH,
        )

    barrier = pltpu.get_barrier_semaphore()

    for i in range(ranks):

        @pl.when(me == i)
        def _(i=i):
            for t in sorted(near[i]):
                pl.semaphore_signal(barrier, inc=1, device_id={"rep": t}, device_id_type=MESH)
            pl.semaphore_wait(barrier, len(near[i]))
            ref = x_ref if i == root else o_ref
            streams = sorted(set(s for s, _ in passes[i]))

            def step(k, carry):
                for s in streams:
                    if i != root:
                        copy(ref, s, k, 0, root).wait_recv()
                    for slot, (t_s, t) in enumerate(passes[i]):
                        if t_s == s:
                            copy(ref, s, k, slot, t).start()
                return carry

            lax.fori_loop(0, chunks, step, 0)

            def rest(k, carry):
                for s in (0, 1):
                    if i == root or s not in streams:
                        copy(ref, s, k, 0, root ^ 1).wait_recv()
                return carry

            lax.fori_loop(0, chunks, rest, 0)
            for slot, (s, t) in enumerate(passes[i]):
                whole = ref.at[:, pl.ds(s * half, half), :]
                pltpu.make_async_remote_copy(
                    src_ref=whole,
                    dst_ref=whole,
                    send_sem=send_sem.at[slot],
                    recv_sem=recv_sem.at[s, 0],
                    device_id={"rep": t},
                    device_id_type=MESH,
                ).wait_send()


def broadcast(shard, owner_index, ranks):
    half = shard.shape[1] // 2
    chunks = max(1, min(32, half // 16))

    def branch(root):
        def call(x):
            return pl.pallas_call(
                functools.partial(bcast_kernel, root, ranks, chunks),
                out_shape=jax.ShapeDtypeStruct(x.shape, x.dtype),
                in_specs=[pl.BlockSpec(memory_space=pl.ANY)],
                out_specs=pl.BlockSpec(memory_space=pl.ANY),
                scratch_shapes=[
                    pltpu.SemaphoreType.DMA((8,)),
                    pltpu.SemaphoreType.DMA((2, chunks)),
                ],
                compiler_params=pltpu.CompilerParams(
                    collective_id=1 + root, has_side_effects=True
                ),
            )(x)

        return call

    return lax.switch(owner_index, [branch(r) for r in range(ranks)], shard)


def attend_kernel(head_group, len_ref, q_ref, ck_ref, cv_ref, pk_ref, pv_ref, o_ref, vone, cone):
    rows = q_ref.shape[0]
    prefix_len = pk_ref.shape[1]
    block = min(1024, prefix_len)
    rate = math.log2(math.e) / math.sqrt(HD)
    vone[:, :HD] = pv_ref[0]
    vone[:, HD:] = jnp.ones((prefix_len, HD), vone.dtype)
    cone[:, :HD] = cv_ref[...]
    cone[:, HD:] = jnp.ones((rows, HD), cone.dtype)
    row_cand = lax.broadcasted_iota(jnp.int32, (rows, rows), 0) // CLEN
    col = lax.broadcasted_iota(jnp.int32, (rows, rows), 1)
    length = jnp.zeros((rows, rows), jnp.int32)
    for c in range(rows // CLEN):
        length = jnp.where(row_cand == c, c * CLEN + len_ref[0, c], length)
    live = (col >= row_cand * CLEN) & (col < length)

    def qk(q, k):
        return lax.dot_general(q, k, (((1,), (1,)), ((), ())), preferred_element_type=jnp.float32)

    def head(g, carry):
        cols = pl.ds(pl.multiple_of(g * HD, HD), HD)
        q = q_ref[:, cols]
        pieces = prefix_len // block
        score = jnp.where(live, qk(q, ck_ref[...]), NEG)
        top = None
        for b in range(pieces + 1):
            if b < pieces:
                ahead = qk(q, pk_ref[0, b * block : (b + 1) * block, :])
            value = cone[...] if b == 0 else vone[(b - 1) * block : b * block, :]
            peak = jnp.max(score, -1, keepdims=True)
            if b == 0:
                top = peak
            else:
                fresh = jnp.maximum(top, peak)
                factor = jnp.exp2((top - fresh) * rate)
                top = fresh
            weight = jnp.exp2((score - top) * rate).astype(jnp.bfloat16)
            part = jnp.dot(weight, value, preferred_element_type=jnp.float32)
            acc = part if b == 0 else acc * factor + part
            score = ahead
        o_ref[:, cols] = (acc[:, :HD] / acc[:, HD:]).astype(o_ref.dtype)
        return carry

    lax.fori_loop(0, head_group, head, 0)


def attend(queries, cand_keys, cand_values, prefix, lengths):
    rows = queries.shape[0]
    kv_heads = cand_keys.shape[1] // HD
    head_group = QH // KVH
    prefix_len = prefix.shape[1]
    wide = head_group * HD
    return pl.pallas_call(
        functools.partial(attend_kernel, head_group),
        grid=(kv_heads,),
        out_shape=jax.ShapeDtypeStruct(queries.shape, jnp.bfloat16),
        in_specs=[
            pl.BlockSpec(memory_space=pltpu.SMEM),
            pl.BlockSpec((rows, wide), lambda h: (0, h)),
            pl.BlockSpec((rows, HD), lambda h: (0, h)),
            pl.BlockSpec((rows, HD), lambda h: (0, h)),
            pl.BlockSpec((1, prefix_len, HD), lambda h: (0, 0, h)),
            pl.BlockSpec((1, prefix_len, HD), lambda h: (1, 0, h)),
        ],
        out_specs=pl.BlockSpec((rows, wide), lambda h: (0, h)),
        scratch_shapes=[
            pltpu.VMEM((prefix_len, 2 * HD), jnp.bfloat16),
            pltpu.VMEM((rows, 2 * HD), jnp.bfloat16),
        ],
    )(lengths, queries, cand_keys, cand_values, prefix, prefix)


def project_kernel(n, tiles, c_ref, w_ref, o_ref, stage, landed, send_sem, recv_sem):
    j = pl.program_id(0)
    me = lax.axis_index("tp")
    rows, width = landed.shape[2], landed.shape[3]

    @pl.when(j == 0)
    def _():
        barrier = pltpu.get_barrier_semaphore()
        for o in range(1, n):
            pl.semaphore_signal(
                barrier, inc=1, device_id={"tp": lax.rem(me + o, n)}, device_id_type=MESH
            )
        pl.semaphore_wait(barrier, n - 1)

    stage[j] = jnp.dot(c_ref[...], w_ref[...], preferred_element_type=jnp.float32).astype(
        stage.dtype
    )

    def copy(t, o):
        peer = lax.rem(me + o, n)
        return pltpu.make_async_remote_copy(
            src_ref=stage.at[t, pl.ds(pl.multiple_of(peer * rows, rows), rows), :],
            dst_ref=landed.at[t, o - 1],
            send_sem=send_sem.at[t, o - 1],
            recv_sem=recv_sem.at[t, o - 1],
            device_id={"tp": peer},
            device_id_type=MESH,
        )

    for o in range(1, n):
        copy(j, o).start()

    def finish(t):
        total = stage[t, pl.ds(pl.multiple_of(me * rows, rows), rows), :].astype(jnp.float32)
        for o in range(1, n):
            copy(t, o).wait_recv()
            total += landed[t, o - 1].astype(jnp.float32)
        o_ref[:, pl.ds(pl.multiple_of(t * width, width), width)] = total.astype(o_ref.dtype)

    @pl.when(j > 0)
    def _():
        finish(j - 1)

    @pl.when(j == tiles - 1)
    def _():
        finish(j)

        def drain(t, carry):
            for o in range(1, n):
                copy(t, o).wait_send()
            return carry

        lax.fori_loop(0, tiles, drain, 0)


def project(context, out_weight, n):
    row_count = context.shape[0]
    rows = row_count // n
    depth, columns = out_weight.shape
    width = min(512, columns)
    tiles = columns // width
    return pl.pallas_call(
        functools.partial(project_kernel, n, tiles),
        grid=(tiles,),
        out_shape=jax.ShapeDtypeStruct((rows, columns), jnp.bfloat16),
        in_specs=[
            pl.BlockSpec((row_count, depth), lambda j: (0, 0)),
            pl.BlockSpec((depth, width), lambda j: (0, j)),
        ],
        out_specs=pl.BlockSpec((rows, columns), lambda j: (0, 0)),
        scratch_shapes=[
            pltpu.VMEM((tiles, row_count, width), jnp.bfloat16),
            pltpu.VMEM((tiles, n - 1, rows, width), jnp.bfloat16),
            pltpu.SemaphoreType.DMA((tiles, n - 1)),
            pltpu.SemaphoreType.DMA((tiles, n - 1)),
        ],
        compiler_params=pltpu.CompilerParams(collective_id=0, has_side_effects=True),
    )(context, out_weight)


def solution(mesh):
    ranks, n = mesh.shape["rep"], mesh.shape["tp"]

    def body(queries, cand_keys, cand_values, prefix_kv, owner, lengths, out_weight):
        arrived = broadcast(prefix_kv[0], owner[0], ranks)
        context = attend(queries, cand_keys, cand_values, arrived, lengths)
        return project(context, out_weight, n)

    in_specs = (
        P("rep", "tp"),
        P("rep", "tp"),
        P("rep", "tp"),
        P("rep", None, None, "tp"),
        P(),
        P("rep", None),
        P("tp", None),
    )
    out_specs = P(("rep", "tp"), None)
    return jax.shard_map(body, mesh=mesh, in_specs=in_specs, out_specs=out_specs, check_vma=False)
```

time: 440 us -> 157 us (0.36)
  waiting for transfers between devices: 189 us -> 0 us
  Pallas kernels: 0 us -> 151 us
  matrix products: 128 us -> 0 us
  other arithmetic: 64.8 us -> 0 us
  local copies, waits for them, and re-layouts: 43.2 us -> 2.29 us
  between operations: 14.1 us -> 0.67 us
    psum x1 -> x0, waiting for transfers between devices: 157 us -> none  [broadcast(): return lax.psum(jnp.where(mine, shard, jnp.zeros_like(shard)), axis)]
    pallas_call x0 -> x3, Pallas kernels: none -> 151 us  [the longest x1 60 us: call(): pl.pallas_call(functools.partial(bcast_kernel, root, ranks, chunks), out_...]
    dot_general x11 -> x0, matrix products: 128 us -> none  [the longest x4 56.1 us: absorb(): jnp.einsum('ipuo,oit->iput', block_expo.astype(jnp.bfloat16), block_value...]
    reduce_sum x5 -> x0, other arithmetic: 58.2 us -> none  [the longest x4 54.8 us: absorb(): new_total = old_total * factor + jnp.sum(block_expo, -1)]
    reduce_scatter x1 -> x0, waiting for transfers between devices: 31.9 us -> none  [body(): lax.psum_scatter(jnp.dot(context, out_weight, preferred_element_type=jnp....]
    while x22 -> x0, local copies, waits for them, and re-layouts: 16 us -> none  [the longest x2 8.4 us: body(): lax.fori_loop(0, block_count, advance, (row_max, row_total, weighted))]
    unnamed x13 -> x1, local copies, waits for them, and re-layouts: 17.2 us -> 2.29 us
    slice x4 -> x0, local copies, waits for them, and re-layouts: 6.86 us -> none  [advance(): return absorb(running, prefix_piece[0], prefix_piece[1])]
  transfers between devices with their start and end apart: 2 -> 0, of which waited for: 2 -> 0; matrix products, arithmetic and copies ran while one was open for 3% -> 0% of each run, Pallas kernels for 0% -> 0%
where the time goes in v1:
time: 157 us; the launch traced here: 154 us
  Pallas kernels  151 us (96%)
  local copies, waits for them, and re-layouts  2.29 us (1%)
    pallas_call x1, Pallas kernels, call(): pl.pallas_call(functools.partial(bcast_kernel, root, ranks, chunks), out_...  60 us
    pallas_call x1, Pallas kernels, attend(): pl.pallas_call(functools.partial(attend_kernel, head_group), grid=(kv_hea...  56.6 us
    pallas_call x1, Pallas kernels, project(): pl.pallas_call(functools.partial(project_kernel, n, tiles), grid=(tiles,)...  34.5 us

profile of v1, /device:TPU:0, one launch (start us, length us, event | category | flops | bytes accessed | tf_op | source)
XLA Modules:
  0.0 154.2 jit_solution(1329853872562972440)
XLA Ops:
  0.7 60.2 %conditional.1 = (bf16[2,4096,512]{2,1,0:T(8,128)(2,1)}) conditional(s32[]{:T(128)} %bitcast, bf16[2,4096,512]{2,1,0:T(8,128)(2,1)} %bitcast.2, bf16[2,4096,512]{2,1,0:T(8,128)(2,1)} %bitcast.3, bf16[2,4096,512]{2,1,0:T(8,128)(2,1)} %bitcast.4, bf16[2,4096,512]{2,1,0:T(8,128)(2,1)} %bitcast.5, ...), branch_computations={%region_0.0_spmd, %region_1.0_spmd, %region_2.0_spmd, %region_3.0_... | conditional | bytes 8 | solution.py:140
  0.7 60.0 %branch_5_fun.1 = bf16[2,4096,512]{2,1,0:T(8,128)(2,1)} custom-call(bf16[2,4096,512]{2,1,0:T(8,128)(2,1)} %x_ref.5), custom_call_target="tpu_custom_call" | custom-call | tf_op jit(solution)/shard_map/cond/branch_5_fun/pallas_call | solution.py:124
  60.9 56.6 %shard_map.73.c_ref = bf16[256,4096]{1,0:T(8,128)(2,1)} custom-call(s32[1,2]{1,0:T(1,128)} %len_ref.1, bf16[256,4096]{1,0:T(8,128)(2,1)} %q_ref.1, bf16[256,512]{1,0:T(8,128)(2,1)} %ck_ref.1, bf16[256,512]{1,0:T(8,128)(2,1)} %cv_ref.1, bf16[2,4096,512]{2,1,0:T(8,128)(2,1)} %get-tuple-element.38.pk_ref.pv_ref, ...), custom_call_target="tpu_custom_call" | custom-call | tf_op jit(solution)/shard_map/pallas_call | solution.py:195
  117.5 34.5 %shard_map.74 = bf16[128,4096]{1,0:T(8,128)(2,1)} custom-call(bf16[256,4096]{1,0:T(8,128)(2,1)} %shard_map.73.c_ref, bf16[4096,4096]{1,0:T(8,128)(2,1)} %w_ref.1), custom_call_target="tpu_custom_call" | custom-call | tf_op jit(solution)/shard_map/pallas_call | solution.py:276
  151.9 2.3 %copy.26 = bf16[128,4096]{1,0:T(8,128)(2,1)} copy(bf16[128,4096]{1,0:T(8,128)(2,1)} %shard_map.74) | data formatting | bytes 2097152

commit v2 on v1

--- a/solution.py
+++ b/solution.py
@@ -183,7 +183,7 @@
         o_ref[:, cols] = (acc[:, :HD] / acc[:, HD:]).astype(o_ref.dtype)
         return carry
 
-    lax.fori_loop(0, head_group, head, 0)
+    lax.fori_loop(0, head_group, head, 0, unroll=2)
 
 
 def attend(queries, cand_keys, cand_values, prefix, lengths):
@@ -251,13 +251,16 @@
             total += landed[t, o - 1].astype(jnp.float32)
         o_ref[:, pl.ds(pl.multiple_of(t * width, width), width)] = total.astype(o_ref.dtype)
 
-    @pl.when(j > 0)
+    lag = min(3, tiles - 1)
+
+    @pl.when(j >= lag)
     def _():
-        finish(j - 1)
+        finish(j - lag)
 
     @pl.when(j == tiles - 1)
     def _():
-        finish(j)
+        for t in range(tiles - lag, tiles):
+            finish(t)
 
         def drain(t, carry):
             for o in range(1, n):

time: 157 us -> 150 us (0.955); the launches traced: 154 us -> 151 us
  Pallas kernels: 151 us -> 148 us
    pallas_call x1, Pallas kernels: 56.6 us -> 53 us  [attend(): pl.pallas_call(functools.partial(attend_kernel, head_group), grid=(kv_hea...]
    pallas_call x1, Pallas kernels: 60 us -> 62.6 us  [call(): pl.pallas_call(functools.partial(bcast_kernel, root, ranks, chunks), out_...]
    pallas_call x1, Pallas kernels: 34.5 us -> 32 us  [project(): pl.pallas_call(functools.partial(project_kernel, n, tiles), grid=(tiles,)...]
where the time goes in v2:
time: 150 us; the launch traced here: 151 us
  Pallas kernels  148 us (99%)
  local copies, waits for them, and re-layouts  2.29 us (2%)
    pallas_call x1, Pallas kernels, call(): pl.pallas_call(functools.partial(bcast_kernel, root, ranks, chunks), out_...  62.6 us
    pallas_call x1, Pallas kernels, attend(): pl.pallas_call(functools.partial(attend_kernel, head_group), grid=(kv_hea...  53 us
    pallas_call x1, Pallas kernels, project(): pl.pallas_call(functools.partial(project_kernel, n, tiles), grid=(tiles,)...  32 us

profile of v2, /device:TPU:0, one launch (start us, length us, event | category | flops | bytes accessed | tf_op | source)
XLA Modules:
  0.0 150.8 jit_solution(12852470473596153432)
XLA Ops:
  0.7 62.8 %conditional.1 = (bf16[2,4096,512]{2,1,0:T(8,128)(2,1)}) conditional(s32[]{:T(128)} %bitcast, bf16[2,4096,512]{2,1,0:T(8,128)(2,1)} %bitcast.2, bf16[2,4096,512]{2,1,0:T(8,128)(2,1)} %bitcast.3, bf16[2,4096,512]{2,1,0:T(8,128)(2,1)} %bitcast.4, bf16[2,4096,512]{2,1,0:T(8,128)(2,1)} %bitcast.5, ...), branch_computations={%region_0.0_spmd, %region_1.0_spmd, %region_2.0_spmd, %region_3.0_... | conditional | bytes 8 | solution.py:140
  0.7 62.6 %branch_11_fun.1 = bf16[2,4096,512]{2,1,0:T(8,128)(2,1)} custom-call(bf16[2,4096,512]{2,1,0:T(8,128)(2,1)} %x_ref.11), custom_call_target="tpu_custom_call" | custom-call | tf_op jit(solution)/shard_map/cond/branch_11_fun/pallas_call | solution.py:124
  63.5 53.0 %shard_map.73.c_ref = bf16[256,4096]{1,0:T(8,128)(2,1)} custom-call(s32[1,2]{1,0:T(1,128)} %len_ref.1, bf16[256,4096]{1,0:T(8,128)(2,1)} %q_ref.1, bf16[256,512]{1,0:T(8,128)(2,1)} %ck_ref.1, bf16[256,512]{1,0:T(8,128)(2,1)} %cv_ref.1, bf16[2,4096,512]{2,1,0:T(8,128)(2,1)} %get-tuple-element.38.pk_ref.pv_ref, ...), custom_call_target="tpu_custom_call" | custom-call | tf_op jit(solution)/shard_map/pallas_call | solution.py:195
  116.5 32.0 %shard_map.74 = bf16[128,4096]{1,0:T(8,128)(2,1)} custom-call(bf16[256,4096]{1,0:T(8,128)(2,1)} %shard_map.73.c_ref, bf16[4096,4096]{1,0:T(8,128)(2,1)} %w_ref.1), custom_call_target="tpu_custom_call" | custom-call | tf_op jit(solution)/shard_map/pallas_call | solution.py:279
  148.5 2.3 %copy.26 = bf16[128,4096]{1,0:T(8,128)(2,1)} copy(bf16[128,4096]{1,0:T(8,128)(2,1)} %shard_map.74) | data formatting | bytes 2097152
